TPU v7x, 256 devices: a whole 4x4x8 slice. The times are simulated.
256 devices in a mesh: segment: 2 (over core), rows: 32 (over z, x), dp: 4 (over y).
Axes of the slice: x: 4, y: 4, z: 8, core: 2. Of those that a mesh axis runs over, the one named last changes fastest.
Arguments:
- coarse: bfloat16 [8, 100, 384, 256], P(('segment', 'dp'), None, 'rows'), may hold values from -6 to 6
- target: bfloat16 [8, 64, 384, 256], P(('segment', 'dp'), None, 'rows'), may hold values from -6 to 6
- noise: bfloat16 [8, 32, 64, 64, 144], P(('segment', 'dp'), 'rows'), may hold values from -6 to 6
- regions: int32 [8, 32, 32, 4], P(('segment', 'dp')), may hold values from 0 to 244, as said below
- reg_conv: bfloat16 [128, 900], replicated, may hold values from -0.1875 to 0.1875
- reg_out: bfloat16 [64, 128], replicated, may hold values from -0.5 to 0.5
- conv_one: bfloat16 [128, 1152], replicated, may hold values from -0.1875 to 0.1875
- conv_two: bfloat16 [128, 1152], replicated, may hold values from -0.1875 to 0.1875
- out_proj: bfloat16 [64, 128], replicated, may hold values from -0.5 to 0.5
- step_embed: float32 [32, 128], replicated, may hold values from -3 to 3
Outputs:
- mean_field: bfloat16 [8, 64, 384, 256], P(('segment', 'dp'), None, 'rows')
- owner_loss: float32 [8, 32], P(('segment', 'dp'), 'rows')
- grad_conv_one: float32 [128, 1152], replicated
- grad_conv_two: float32 [128, 1152], replicated
- grad_out_proj: float32 [64, 128], replicated
- grad_embed: float32 [32, 128], replicated
Inputs may be any that keep to these rules, and one draw needn't show every extreme that they name: `regions`: for sample s, strip i and entry k: entry 0 is the patch's row offset within strip i (0 on the last strip), entry 1 its first column, at most 244, entry 2 its owner, entry 3 its noise level below 32. Every owner receives 2 * 32, 32 or 16 patches of a sample; for each owner with 64 there is one with 32 and two with 16. No strip lists more than 2 patches for one owner, and some strip lists exactly 2 for one owner.
All inputs are finite; a program needn't handle non-finite values.
Results may differ from a plain program's by a relative error of at most 0.0048.
Values may be sent and summed in bfloat16 or wider, within the bound.
A program may use at most 192 MiB of HBM per device.

v0:
```python
import math
import jax
import jax.numpy as jnp
from jax import lax
from jax.sharding import PartitionSpec as P

PATCH = 12
TAPS = ((-1, -1), (-1, 0), (-1, 1), (0, -1), (0, 0), (0, 1), (1, -1), (1, 0), (1, 1))


def padded_2(cells, sides, width):
    for axis, dim in sides:
        count = lax.axis_size(axis)
        ends = count - 1
        head = lax.slice_in_dim(cells, 0, width, axis=dim)
        tail = lax.slice_in_dim(cells, cells.shape[dim] - width, cells.shape[dim], axis=dim)
        cells = jnp.concatenate(
            [
                lax.ppermute(tail, axis, [(i, (i + 1) % count) for i in range(ends)]),
                cells,
                lax.ppermute(head, axis, [((i + 1) % count, i) for i in range(ends)]),
            ],
            axis=dim,
        )
    return cells


def shifted_2(block, axis, distance):
    devices = range(lax.axis_size(axis))
    route = [(i - distance, i) for i in devices if i - distance in devices]
    return lax.ppermute(block, axis, route)


def shifted(values, row_step, col_step, stride):
    length = values.shape[-1]
    margin = stride + 1
    widths = [(0, 0)] * (values.ndim - 1) + [(margin, margin)]
    padded = jnp.pad(values, widths)
    offset = margin + row_step * stride + col_step
    moved = lax.slice_in_dim(padded, offset, offset + length, axis=values.ndim - 1)
    column = jnp.arange(length, dtype=jnp.int32) % stride + col_step
    inside = (column >= 0) & (column < stride)
    return jnp.where(inside, moved, jnp.zeros((), moved.dtype))


def columns(values, stride):
    return jnp.concatenate(
        [shifted(values, row_step, col_step, stride) for row_step, col_step in TAPS], axis=-2
    )


def fold(gradients, stride):
    width = gradients.shape[-2] // 9
    result = jnp.zeros(gradients.shape[:-2] + (width, gradients.shape[-1]), jnp.float32)
    for position, (row_step, col_step) in enumerate(TAPS):
        piece = gradients[..., position * width : (position + 1) * width, :]
        result = result + shifted(piece, -row_step, -col_step, stride)
    return result


def noise_levels(level_count):
    steps_f = jnp.arange(level_count, dtype=jnp.float32)
    return 0.1 * jnp.exp(steps_f * (math.log(100.0) / (level_count - 1)))


def silu_slope(values):
    gate = jax.nn.sigmoid(values)
    return gate * (1.0 + values * (1.0 - gate))


def product(form, left, right):
    return jnp.einsum(form, left, right, preferred_element_type=jnp.float32)


def regress(grid_rows, reg_conv, reg_out):
    channels, height, width = grid_rows.shape
    flat = grid_rows.reshape(channels, height * width)
    hidden = product("ok,kp->op", reg_conv, columns(flat, width))
    activated = jax.nn.silu(hidden).astype(jnp.bfloat16)
    mean_flat = product("co,op->cp", reg_out, activated).astype(jnp.bfloat16)
    return mean_flat.reshape(reg_out.shape[0], height, width)


def patch_block(mean_part, target_part, noise_part, step_ids, in_use, weights):
    conv_one, conv_two, out_proj, step_embed = weights
    stride = PATCH
    level_count = step_embed.shape[0]
    sigma_table = noise_levels(level_count)
    step_hot = (step_ids[:, None] == jnp.arange(level_count, dtype=jnp.int32)[None, :]).astype(
        jnp.float32
    )
    sigma = jnp.sum(step_hot * sigma_table[None, :], axis=1)
    sigma_sq = sigma * sigma + 1.0
    scale_in = (1.0 / jnp.sqrt(sigma_sq))[:, None, None]
    scale_skip = (1.0 / sigma_sq)[:, None, None]
    scale_out = (sigma / jnp.sqrt(sigma_sq))[:, None, None]
    weight_loss = sigma_sq / (sigma * sigma)
    mean_float = mean_part.astype(jnp.float32)
    residual = target_part.astype(jnp.float32) - mean_float
    noisy = residual + sigma[:, None, None] * noise_part.astype(jnp.float32)
    inputs = jnp.concatenate([scale_in * noisy, mean_float], axis=1).astype(jnp.bfloat16)
    cols_in = columns(inputs, stride)
    embedded = jnp.sum(step_hot[:, :, None] * step_embed[None, :, :], axis=1)
    pre_one = product("ok,bkp->bop", conv_one, cols_in) + embedded[:, :, None]
    act_one = jax.nn.silu(pre_one).astype(jnp.bfloat16)
    cols_one = columns(act_one, stride)
    pre_two = product("ok,bkp->bop", conv_two, cols_one)
    act_two = jax.nn.silu(pre_two).astype(jnp.bfloat16)
    output = product("co,bop->bcp", out_proj, act_two)
    error = scale_skip * noisy + scale_out * output - residual
    losses = weight_loss * jnp.mean(error * error, axis=(1, 2)) * in_use
    factor = 2.0 * weight_loss * in_use / (error.shape[1] * error.shape[2])
    grad_output = (factor[:, None, None] * scale_out * error).astype(jnp.bfloat16)
    grad_proj = product("bcp,bop->co", grad_output, act_two)
    grad_act_two = product("co,bcp->bop", out_proj, grad_output)
    grad_pre_two = (grad_act_two * silu_slope(pre_two)).astype(jnp.bfloat16)
    grad_two = product("bop,bkp->ok", grad_pre_two, cols_one)
    grad_cols = product("ok,bop->bkp", conv_two, grad_pre_two)
    grad_act_one = fold(grad_cols, stride)
    grad_pre_one = (grad_act_one * silu_slope(pre_one)).astype(jnp.bfloat16)
    grad_one = product("bop,bkp->ok", grad_pre_one, cols_in)
    pixel_sums = jnp.sum(grad_pre_one, axis=2, dtype=jnp.float32)
    grad_table = jnp.sum(step_hot[:, :, None] * pixel_sums[:, None, :], axis=0)
    return (losses, (grad_one, grad_two, grad_proj, grad_table))


def run_blocks(mean_part, target_part, noise_part, step_ids, in_use, weights):
    patch_count = mean_part.shape[0]
    blocks = patch_count // 4

    def regroup(values):
        return values.reshape((blocks, 4) + values.shape[1:])

    def advance(running, group_block):
        losses, gradients = patch_block(
            group_block[0], group_block[1], group_block[2], group_block[3], group_block[4], weights
        )
        summed = (
            running[0] + gradients[0],
            running[1] + gradients[1],
            running[2] + gradients[2],
            running[3] + gradients[3],
        )
        return (summed, losses)

    initial = (
        jnp.zeros(weights[0].shape, jnp.float32),
        jnp.zeros(weights[1].shape, jnp.float32),
        jnp.zeros(weights[2].shape, jnp.float32),
        jnp.zeros(weights[3].shape, jnp.float32),
    )
    stacked = (
        regroup(mean_part),
        regroup(target_part),
        regroup(noise_part),
        regroup(step_ids),
        regroup(in_use),
    )
    gradients, losses = lax.scan(advance, initial, stacked)
    return (losses.reshape(patch_count), gradients)


def owner_tables(region_rows, strips):
    owners = region_rows[:, :, 2]
    owner_hot = (owners[:, :, None] == jnp.arange(strips, dtype=jnp.int32)[None, None, :]).astype(
        jnp.int32
    )
    pair_rank = jnp.sum((jnp.cumsum(owner_hot, axis=1) - owner_hot) * owner_hot, axis=2)
    flat_hot = owner_hot.reshape(-1, strips)
    owner_slot = jnp.sum((jnp.cumsum(flat_hot, axis=0) - flat_hot) * flat_hot, axis=1).reshape(
        owners.shape
    )
    return (owners, pair_rank, owner_slot)


def owned_slots(region_rows, owners, pair_rank, owner_slot, strip_index, capacity, most, height):
    strips = region_rows.shape[0]
    slot_hits = (
        (owners == strip_index)[:, :, None]
        & (owner_slot[:, :, None] == jnp.arange(most, dtype=jnp.int32)[None, None, :])
    ).astype(jnp.int32)
    strip_ids = jnp.arange(strips, dtype=jnp.int32)[:, None]
    recv_index = jnp.sum(slot_hits * (strip_ids * capacity + pair_rank)[:, :, None], axis=(0, 1))
    in_use = jnp.sum(slot_hits, axis=(0, 1)).astype(jnp.float32)
    step_ids = jnp.sum(slot_hits * region_rows[:, :, 3][:, :, None], axis=(0, 1))
    row_at = jnp.sum(
        slot_hits * (strip_ids * height + region_rows[:, :, 0])[:, :, None], axis=(0, 1)
    )
    col_at = jnp.sum(slot_hits * region_rows[:, :, 1][:, :, None], axis=(0, 1))
    return (recv_index, in_use, step_ids, row_at, col_at)


def cut_patches(source_grid, row_at, col_at, height):
    zero_index = jnp.zeros((), jnp.int32)

    def cut(row_start, col_start):
        piece = lax.dynamic_slice(
            source_grid,
            (zero_index, zero_index, row_start, col_start),
            (2, source_grid.shape[1], height, height),
        )
        return piece.reshape(2, source_grid.shape[1], height * height)

    return jax.vmap(cut)(row_at, col_at)


def per_device(
    coarse, target, noise, regions, reg_conv, reg_out, conv_one, conv_two, out_proj, step_embed
):
    strips = lax.axis_size("rows")
    strip_index = lax.axis_index("rows")
    region_rows = regions[0]
    per_strip = region_rows.shape[1]
    capacity = max(2, (2 * per_strip + strips - 1) // strips)
    most = 2 * per_strip
    weights = (conv_one, conv_two, out_proj, step_embed)
    rimmed = padded_2(coarse, (("rows", 2),), 1)
    mean_strip = regress(rimmed[0], reg_conv, reg_out)[:, 1:-1]
    height = mean_strip.shape[1]
    pair_strip = jnp.stack([mean_strip, target[0]])
    owners, pair_rank, owner_slot = owner_tables(region_rows, strips)
    own_regions = lax.dynamic_index_in_dim(region_rows, strip_index, 0, keepdims=False)
    own_pairs = lax.dynamic_index_in_dim(pair_rank, strip_index, 0, keepdims=False)
    slot_noise = noise[0, 0]
    below = shifted_2(pair_strip[:, :, : height - 1], "rows", -1)
    extended = jnp.concatenate([pair_strip, below], axis=2)
    patches = cut_patches(extended, own_regions[:, 0], own_regions[:, 1], height)
    outgoing = jnp.zeros((strips, capacity) + patches.shape[1:], patches.dtype)
    outgoing = outgoing.at[own_regions[:, 2], own_pairs].set(patches)
    received = lax.all_to_all(outgoing, "rows", split_axis=0, concat_axis=0, tiled=True)
    flat_recv = received.reshape((strips * capacity,) + patches.shape[1:])
    recv_index, in_use, step_ids, row_at, col_at = owned_slots(
        region_rows, owners, pair_rank, owner_slot, strip_index, capacity, most, height
    )
    gathered = jnp.take(flat_recv, recv_index, axis=0)
    losses, gradients = run_blocks(
        gathered[:, 0], gathered[:, 1], slot_noise, step_ids, in_use, weights
    )
    owner_total = jnp.sum(losses)
    totals = lax.psum(
        (gradients[0], gradients[1], gradients[2], gradients[3]), ("segment", "rows", "dp")
    )
    return (mean_strip[None], owner_total.reshape(1, 1), totals[0], totals[1], totals[2], totals[3])


def solution(mesh):
    placed = (
        P(("segment", "dp"), None, "rows", None),
        P(("segment", "dp"), None, "rows", None),
        P(("segment", "dp"), "rows", None, None, None),
        P(("segment", "dp"), None, None, None),
        P(),
        P(),
        P(),
        P(),
        P(),
        P(),
    )
    return jax.shard_map(
        per_device,
        mesh=mesh,
        in_specs=placed,
        out_specs=(
            P(("segment", "dp"), None, "rows", None),
            P(("segment", "dp"), "rows"),
            P(),
            P(),
            P(),
            P(),
        ),
        check_vma=False,
    )
```

profile of v0, /device:TPU:8, one launch (start us, length us, event | category | flops | bytes accessed | tf_op | source)
XLA Modules:
  0.0 851.5 jit_solution(5382771631686754666)
XLA Ops:
  8.1 3.4 collective-permute-start
  12.8 3.2 copy.114
  18.2 4.4 slice_select_fusion.1
  22.6 41.7 %concatenate.38 = bf16[900,3584]{1,0:T(8,128)(2,1)} concatenate(bf16[100,3584]{1,0:T(8,128)(2,1)} %get-tuple-element.387, bf16[100,3584]{1,0:T(8,128)(2,1)} %get-tuple-element.390, bf16[100,3584]{1,0:T(8,128)(2,1)} %get-tuple-element.380, bf16[100,3584]{1,0:T(8,128)(2,1)} %get-tuple-element.388, bf16[100,3584]{1,0:T(8,128)(2,1)} %get-tuple-element.391, ...), dimensions={0} | concatenate | bytes 12902400 | tf_op jit(solution)/shard_map/concatenate | solution.py:47
  64.3 5.4 fusion.29
  71.2 3.2 copy.113
  74.4 4.9 pad_maximum_fusion.2
  79.3 4.6 copy.115
  87.4 16.4 %collective-permute-done.2 = bf16[2,64,11,256]{3,1,2,0:T(8,128)(2,1)} collective-permute-done((bf16[2,64,11,256]{3,1,2,0:T(8,128)(2,1)}, bf16[2,64,11,256]{3,1,2,0:T(8,128)(2,1)}, u32[]{:S(2)}, u32[]{:S(2)}) %collective-permute-start.2) | collective-permute-done | bytes 720928 | tf_op jit(solution)/shard_map/ppermute | solution.py:31
  103.8 4.7 copy.116
  108.4 8.1 pad_maximum_fusion.1
  116.5 8.6 %gather_fusion = bf16[32,2,64,12,12]{2,1,4,3,0:T(2,128)(2,1)S(1)} fusion(bf16[2,64,23,256]{1,0,3,2:T(2,128)(2,1)} %pad_maximum_fusion.1, s32[32]{0:T(128)S(1)} %get-tuple-element.398), kind=kCustom, calls=%fused_computation | custom fusion | bytes 2359808 | tf_op jit(solution)/shard_map/vmap()/gather | solution.py:197
  125.2 3.9 copy.117
  131.6 5.7 scatter_fusion
  137.3 15.6 %all-to-all-start = ((bf16[32,2,2,64,144]{4,3,2,1,0:T(8,128)(2,1)}), bf16[32,2,2,64,144]{4,3,2,1,0:T(8,128)(2,1)}, u32[]{:S(2)}, u32[]{:S(2)}) async-start(bf16[32,2,2,64,144]{4,3,2,1,0:T(8,128)(2,1)} %scatter_fusion), calls=%async_computation | async-start | bytes 8388608 | tf_op jit(solution)/shard_map/all_to_all | solution.py:230
  153.4 9.0 %reduce-window.6 = s32[32,8,128]{2,1,0:T(8,128)S(1)} reduce-window(s32[32,8,128]{2,1,0:T(8,128)S(1)} %fusion.38, s32[]{:T(128)} %constant.269.clone.1), window={size=1x1x128 pad=0_0x0_0x127_0}, to_apply=%region_0.1 | reduce-window | flops 4161536 | bytes 262148 | tf_op jit(solution)/shard_map/reduce-window
  164.0 81.0 %all-to-all-done = bf16[32,2,2,64,144]{4,3,2,1,0:T(8,128)(2,1)} async-done(((bf16[32,2,2,64,144]{4,3,2,1,0:T(8,128)(2,1)}), bf16[32,2,2,64,144]{4,3,2,1,0:T(8,128)(2,1)}, u32[]{:S(2)}, u32[]{:S(2)}) %all-to-all-start) | async-done | bytes 2359328 | tf_op jit(solution)/shard_map/all_to_all | solution.py:230
  245.0 5.0 gather_fusion.1
  255.2 328.0 %while.21 = (s32[]{:T(128)}, f32[128,1152]{1,0:T(8,128)}, f32[128,1152]{1,0:T(8,128)}, f32[64,128]{1,0:T(8,128)S(1)}, f32[32,128]{1,0:T(8,128)S(1)}, /*index=5*/...) while((s32[]{:T(128)}, f32[128,1152]{1,0:T(8,128)}, ...), condition=%wide.region_15.16_spmd.clone, body=%wide.region_9.15_spmd.clone.sunk | while | flops 884677568 | bytes 48410204 | solution.py:159
  286.9 2.8 fusion.117
  348.6 2.8 fusion.117
  533.7 2.8 fusion.117
  584.5 74.9 %all-reduce.11 = (f32[64,128]{1,0:T(8,128)}, f32[32,128]{1,0:T(8,128)}) all-reduce(f32[64,128]{1,0:T(8,128)S(1)} %get-tuple-element.201, f32[32,128]{1,0:T(8,128)S(1)} %get-tuple-element.202), channel_id=1, replica_groups=mesh['segment'=2,'rows'=32,'dp'=4] {'segment','rows','dp'}, use_global_device_ids=true, to_apply=%region_19.20 | all-reduce | flops 12288 | bytes 98304 | tf_op jit(solution)/shard_map/psum | solution.py:240
  659.4 181.4 %all-reduce.15.cloned.1.call-done = (f32[128,1152]{1,0:T(8,128)}, f32[128,1152]{1,0:T(8,128)}) async-done(((f32[128,1152]{1,0:T(8,128)}, f32[128,1152]{1,0:T(8,128)}), (f32[128,1152]{1,0:T(8,128)}, f32[128,1152]{1,0:T(8,128)})) %all-reduce.15.cloned.1.call-update) | async-done | bytes 1179664 | tf_op jit(solution)/shard_map/psum | solution.py:240
  (917 shorter events, 339.3 us)
Async XLA Ops:
  7.2 57.2 %copy-start = (bf16[128,900]{0,1:T(8,128)(2,1)S(1)}, bf16[128,900]{0,1:T(8,128)(2,1)}, u32[]{:S(2)}) copy-start(bf16[128,900]{0,1:T(8,128)(2,1)} %param.16) | copy-start | bytes 691204
  7.2 10.4 %copy-start.9 = (bf16[1,100,12,256]{3,1,2,0:T(8,128)(2,1)S(1)}, bf16[1,100,12,256]{3,1,2,0:T(8,128)(2,1)}, u32[]{:S(2)}) copy-start(bf16[1,100,12,256]{3,1,2,0:T(8,128)(2,1)} %param.12) | copy-start | bytes 1843204
  8.1 8.8 %collective-permute-start = (bf16[1,100,1,256]{3,1,2,0:T(8,128)(2,1)S(1)}, bf16[1,100,1,256]{3,1,2,0:T(8,128)(2,1)S(1)}, u32[]{:S(2)}, u32[]{:S(2)}) collective-permute-start(bf16[1,100,1,256]{3,1,2,0:T(8,128)(2,1)S(1)} %get-tuple-element.393), channel_id=1, source_target_pairs={{0,4},{4,8},{8,12},{12,16},{16,20},{20,24},{24,28},{28,32},{32,36}... | collective-permute-start | bytes 153608 | tf_op jit(solution)/shard_map/ppermute | solution.py:19
  11.5 6.0 collective-permute-start.1
  22.6 41.7 %copy-start.12 = (bf16[64,128]{1,0:T(8,128)(2,1)S(1)}, bf16[64,128]{1,0:T(8,128)(2,1)}, u32[]{:S(2)}) copy-start(bf16[64,128]{1,0:T(8,128)(2,1)} %param.17) | copy-start | bytes 49156
  83.9 19.9 %collective-permute-start.2 = (bf16[2,64,11,256]{3,1,2,0:T(8,128)(2,1)}, bf16[2,64,11,256]{3,1,2,0:T(8,128)(2,1)}, u32[]{:S(2)}, u32[]{:S(2)}) collective-permute-start(bf16[2,64,11,256]{3,1,2,0:T(8,128)(2,1)} %copy.115), channel_id=1, source_target_pairs={{4,0},{8,4},{12,8},{16,12},{20,16},{24,20},{28,24},{32,28},{36,32}... | collective-permute-start | bytes 2162696 | tf_op jit(solution)/shard_map/ppermute | solution.py:31
  137.3 107.7 %all-to-all-start = ((bf16[32,2,2,64,144]{4,3,2,1,0:T(8,128)(2,1)}), bf16[32,2,2,64,144]{4,3,2,1,0:T(8,128)(2,1)}, u32[]{:S(2)}, u32[]{:S(2)}) async-start(bf16[32,2,2,64,144]{4,3,2,1,0:T(8,128)(2,1)} %scatter_fusion), calls=%async_computation | async-start | bytes 8388608 | tf_op jit(solution)/shard_map/all_to_all | solution.py:230
  152.9 687.9 %all-reduce.15.cloned.1.call-start = ((), (), s32[]{:S(2)}) async-start(), calls=%async_computation.1 | async-start | bytes 2359296 | tf_op jit(solution)/shard_map/psum | solution.py:240
  262.6 2.9 copy-start.2
  282.1 2.9 copy-start.2
  302.7 2.9 copy-start.2
  323.3 2.9 copy-start.2
  343.8 2.9 copy-start.2
  364.4 2.9 copy-start.2
  385.0 2.9 copy-start.2
  405.5 2.9 copy-start.2
  426.1 2.9 copy-start.2
  446.6 2.9 copy-start.2
  467.2 2.9 copy-start.2
  487.8 2.9 copy-start.2
  508.3 2.9 copy-start.2
  528.9 2.9 copy-start.2
  570.0 2.9 copy-start.2
  583.2 261.5 %copy-start.1 = (bf16[128,900]{0,1:T(8,128)(2,1)S(1)}, bf16[128,900]{0,1:T(8,128)(2,1)}, u32[]{:S(2)}) copy-start(bf16[128,900]{0,1:T(8,128)(2,1)} %param.16) | copy-start | bytes 691204
  (69 other events, 102.8 us)
Sparse Core Ops, SparseCore 0:
  583.3 257.4 all-reduce.14
where the time goes:
time: 859 us; the launch traced here: 851 us
  waiting for transfers between devices  279 us (32%)
  matrix products  190 us (22%)
  local copies, waits for them, and re-layouts  148 us (17%)
  other arithmetic  119 us (14%)
  blocking collectives  74.9 us (9%)
  starting transfers between devices  22 us (3%)
  between operations  14.3 us (2%)
    dot_general x129, matrix products, product(): return jnp.einsum(form, left, right, preferred_element_type=jnp.float32)  190 us
    psum x1, waiting for transfers between devices, per_device(): lax.psum((gradients[0], gradients[1], gradients[2], gradients[3]), ('segm...  181 us
    all_to_all x1, waiting for transfers between devices, per_device(): lax.all_to_all(outgoing, 'rows', split_axis=0, concat_axis=0, tiled=True)  81 us
    psum x1, blocking collectives, per_device(): lax.psum((gradients[0], gradients[1], gradients[2], gradients[3]), ('segm...  74.9 us
    concatenate x1, local copies, waits for them, and re-layouts, columns(): jnp.concatenate([shifted(values, row_step, col_step, stride) for row_step...  41.7 us
    while x256, other arithmetic  34.1 us
    another operation x19, other arithmetic  27.5 us
    dynamic_update_slice x16, local copies, waits for them, and re-layouts, run_blocks(): gradients, losses = lax.scan(advance, initial, stacked)  21.3 us
  transfers between devices with their start and end apart: 5, of which 4 were waited for; matrix products, arithmetic and copies ran while one was open for 2% of the time, Pallas kernels for 0%

commit v1 on v0

--- a/solution.py
+++ b/solution.py
@@ -237,9 +237,9 @@
         gathered[:, 0], gathered[:, 1], slot_noise, step_ids, in_use, weights
     )
     owner_total = jnp.sum(losses)
-    totals = lax.psum(
-        (gradients[0], gradients[1], gradients[2], gradients[3]), ("segment", "rows", "dp")
-    )
+    totals = (gradients[0], gradients[1], gradients[2], gradients[3])
+    for num in (("rows", "dp"), "segment"):
+        totals = jax.lax.psum(totals, num)
     return (mean_strip[None], owner_total.reshape(1, 1), totals[0], totals[1], totals[2], totals[3])
 
 

time: 859 us -> 1500 us (1.75)
  blocking collectives: 74.9 us -> 683 us
  waiting for transfers between devices: 279 us -> 318 us
    psum x1 -> x2, blocking collectives: 74.9 us -> 683 us  [per_device(): totals = jax.lax.psum(totals, num)]
    psum x1 -> x2, waiting for transfers between devices: 181 us -> 220 us  [per_device(): totals = jax.lax.psum(totals, num)]
    dynamic_update_slice x16, local copies, waits for them, and re-layouts: 21.3 us -> 0.61 us  [run_blocks(): gradients, losses = lax.scan(advance, initial, stacked)]
  transfers between devices with their start and end apart: 5 -> 6, of which waited for: 4 -> 4; matrix products, arithmetic and copies ran while one was open for 2% -> 1% of each run, Pallas kernels for 0% -> 0%
where the time goes in v1:
time: 1500 us; the launch traced here: 1490 us
  blocking collectives  683 us (46%)
  waiting for transfers between devices  318 us (21%)
  matrix products  190 us (13%)
  local copies, waits for them, and re-layouts  138 us (9%)
  other arithmetic  118 us (8%)
  starting transfers between devices  22 us (1%)
    psum x2, blocking collectives, per_device(): totals = jax.lax.psum(totals, num)  683 us
    psum x2, waiting for transfers between devices, per_device(): totals = jax.lax.psum(totals, num)  220 us
    dot_general x129, matrix products, product(): return jnp.einsum(form, left, right, preferred_element_type=jnp.float32)  190 us
    all_to_all x1, waiting for transfers between devices, per_device(): lax.all_to_all(outgoing, 'rows', split_axis=0, concat_axis=0, tiled=True)  81 us
    concatenate x1, local copies, waits for them, and re-layouts, columns(): jnp.concatenate([shifted(values, row_step, col_step, stride) for row_step...  41.7 us
    while x256, other arithmetic  34.1 us
  transfers between devices with their start and end apart: 6, of which 4 were waited for; matrix products, arithmetic and copies ran while one was open for 1% of the time, Pallas kernels for 0%

profile of v1, /device:TPU:8, one launch (start us, length us, event | category | flops | bytes accessed | tf_op | source)
XLA Modules:
  0.0 1487.1 jit_solution(7167613610635365401)
XLA Ops:
  8.1 3.4 collective-permute-start
  12.8 3.2 copy.114
  18.2 4.4 slice_select_fusion.1
  22.6 41.7 %concatenate.38 = bf16[900,3584]{1,0:T(8,128)(2,1)} concatenate(bf16[100,3584]{1,0:T(8,128)(2,1)} %get-tuple-element.391, bf16[100,3584]{1,0:T(8,128)(2,1)} %get-tuple-element.394, bf16[100,3584]{1,0:T(8,128)(2,1)} %get-tuple-element.384, bf16[100,3584]{1,0:T(8,128)(2,1)} %get-tuple-element.392, bf16[100,3584]{1,0:T(8,128)(2,1)} %get-tuple-element.395, ...), dimensions={0} | concatenate | bytes 12902400 | tf_op jit(solution)/shard_map/concatenate | solution.py:47
  64.3 5.4 fusion.29
  71.2 3.2 copy.113
  74.4 4.9 pad_maximum_fusion.2
  79.3 4.6 copy.115
  87.4 16.4 %collective-permute-done.2 = bf16[2,64,11,256]{3,1,2,0:T(8,128)(2,1)} collective-permute-done((bf16[2,64,11,256]{3,1,2,0:T(8,128)(2,1)}, bf16[2,64,11,256]{3,1,2,0:T(8,128)(2,1)}, u32[]{:S(2)}, u32[]{:S(2)}) %collective-permute-start.2) | collective-permute-done | bytes 720928 | tf_op jit(solution)/shard_map/ppermute | solution.py:31
  103.8 4.7 copy.116
  108.4 8.1 pad_maximum_fusion.1
  116.5 8.6 gather_fusion
  125.2 3.9 copy.117
  131.6 5.7 scatter_fusion
  137.3 15.6 %all-to-all-start = ((bf16[32,2,2,64,144]{4,3,2,1,0:T(8,128)(2,1)}), bf16[32,2,2,64,144]{4,3,2,1,0:T(8,128)(2,1)}, u32[]{:S(2)}, u32[]{:S(2)}) async-start(bf16[32,2,2,64,144]{4,3,2,1,0:T(8,128)(2,1)} %scatter_fusion), calls=%async_computation | async-start | bytes 8388608 | tf_op jit(solution)/shard_map/all_to_all | solution.py:230
  153.4 9.0 reduce-window.6
  164.0 81.0 %all-to-all-done = bf16[32,2,2,64,144]{4,3,2,1,0:T(8,128)(2,1)} async-done(((bf16[32,2,2,64,144]{4,3,2,1,0:T(8,128)(2,1)}), bf16[32,2,2,64,144]{4,3,2,1,0:T(8,128)(2,1)}, u32[]{:S(2)}, u32[]{:S(2)}) %all-to-all-start) | async-done | bytes 2359328 | tf_op jit(solution)/shard_map/all_to_all | solution.py:230
  245.0 5.0 gather_fusion.1
  255.2 317.5 %while.21 = (s32[]{:T(128)}, f32[128,1152]{1,0:T(8,128)}, f32[128,1152]{1,0:T(8,128)}, f32[64,128]{1,0:T(8,128)S(1)}, f32[32,128]{1,0:T(8,128)S(1)}, /*index=5*/...) while((s32[]{:T(128)}, f32[128,1152]{1,0:T(8,128)}, ...), condition=%wide.region_15.16_spmd.clone, body=%wide.region_9.15_spmd.clone.sunk | while | flops 884677568 | bytes 48410204 | solution.py:159
  286.3 2.8 fusion.117
  306.2 2.8 fusion.117
  572.7 219.7 %all-reduce.18.cloned.1.call-done = (f32[128,1152]{1,0:T(8,128)}, f32[128,1152]{1,0:T(8,128)}) async-done(((f32[128,1152]{1,0:T(8,128)}, f32[128,1152]{1,0:T(8,128)}), (f32[128,1152]{1,0:T(8,128)}, f32[128,1152]{1,0:T(8,128)})) %all-reduce.18.cloned.1.call-update) | async-done | bytes 1179664 | tf_op jit(solution)/shard_map/psum | solution.py:242
  793.0 679.3 %all-reduce.11 = (f32[64,128]{1,0:T(8,128)S(1)}, f32[32,128]{1,0:T(8,128)S(1)}) all-reduce(f32[64,128]{1,0:T(8,128)S(1)} %get-tuple-element.201, f32[32,128]{1,0:T(8,128)S(1)} %get-tuple-element.202), channel_id=1, replica_groups=mesh['segment'=2,'rows'=32,'dp'=4] {'rows','dp'}, use_global_device_ids=true, to_apply=%region_21.22 | all-reduce | flops 12288 | bytes 98304 | tf_op jit(solution)/shard_map/psum | solution.py:242
  1472.3 4.1 all-reduce.13
  (921 shorter events, 330.9 us)
Async XLA Ops:
  7.2 57.2 %copy-start = (bf16[128,900]{0,1:T(8,128)(2,1)S(1)}, bf16[128,900]{0,1:T(8,128)(2,1)}, u32[]{:S(2)}) copy-start(bf16[128,900]{0,1:T(8,128)(2,1)} %param.16) | copy-start | bytes 691204
  7.2 10.4 copy-start.9
  8.1 8.8 collective-permute-start
  11.5 6.0 collective-permute-start.1
  22.6 41.7 %copy-start.12 = (bf16[64,128]{1,0:T(8,128)(2,1)S(1)}, bf16[64,128]{1,0:T(8,128)(2,1)}, u32[]{:S(2)}) copy-start(bf16[64,128]{1,0:T(8,128)(2,1)} %param.17) | copy-start | bytes 49156
  83.9 19.9 %collective-permute-start.2 = (bf16[2,64,11,256]{3,1,2,0:T(8,128)(2,1)}, bf16[2,64,11,256]{3,1,2,0:T(8,128)(2,1)}, u32[]{:S(2)}, u32[]{:S(2)}) collective-permute-start(bf16[2,64,11,256]{3,1,2,0:T(8,128)(2,1)} %copy.115), channel_id=1, source_target_pairs={{4,0},{8,4},{12,8},{16,12},{20,16},{24,20},{28,24},{32,28},{36,32}... | collective-permute-start | bytes 2162696 | tf_op jit(solution)/shard_map/ppermute | solution.py:31
  137.3 107.7 %all-to-all-start = ((bf16[32,2,2,64,144]{4,3,2,1,0:T(8,128)(2,1)}), bf16[32,2,2,64,144]{4,3,2,1,0:T(8,128)(2,1)}, u32[]{:S(2)}, u32[]{:S(2)}) async-start(bf16[32,2,2,64,144]{4,3,2,1,0:T(8,128)(2,1)} %scatter_fusion), calls=%async_computation | async-start | bytes 8388608 | tf_op jit(solution)/shard_map/all_to_all | solution.py:230
  152.9 639.5 %all-reduce.18.cloned.1.call-start = ((), (), s32[]{:S(2)}) async-start(), calls=%async_computation.1 | async-start | bytes 2359296 | tf_op jit(solution)/shard_map/psum | solution.py:242
  262.6 2.9 copy-start.2
  281.5 2.9 copy-start.2
  301.4 2.9 copy-start.2
  321.3 2.9 copy-start.2
  341.2 2.9 copy-start.2
  361.1 2.9 copy-start.2
  381.0 2.9 copy-start.2
  400.9 2.9 copy-start.2
  420.8 2.9 copy-start.2
  440.7 2.9 copy-start.2
  460.7 2.9 copy-start.2
  480.6 2.9 copy-start.2
  500.5 2.9 copy-start.2
  540.3 2.9 copy-start.2
  572.6 907.6 %copy-start.1 = (bf16[128,900]{0,1:T(8,128)(2,1)S(1)}, bf16[128,900]{0,1:T(8,128)(2,1)}, u32[]{:S(2)}) copy-start(bf16[128,900]{0,1:T(8,128)(2,1)} %param.16) | copy-start | bytes 691204
  572.7 903.7 %all-reduce.20.cloned.1.call-start = ((), (), s32[]{:S(2)}) async-start(), calls=%async_computation.2 | async-start | bytes 2359296 | tf_op jit(solution)/shard_map/psum | solution.py:242
  (70 other events, 95.3 us)
Sparse Core Ops, SparseCore 0:
  572.8 219.5 all-reduce.17
  795.0 27.9 all-reduce.19
